TPU v7x, 32 devices: a whole 2x2x4 slice. The times are simulated.
32 devices in a mesh: dp: 8 (over z, x), feat: 4 (over y, core).
Axes of the slice: x: 2, y: 2, z: 4, core: 2. Of those that a mesh axis runs over, the one named last changes fastest.
Arguments:
- member_feats: bfloat16 [32768, 256], P(('dp', 'feat')), may hold values from -6 to 6
- labels: int32 [32768], P(('dp', 'feat')), may hold values 0 or 1
- fixed_values: bfloat16 [32768, 2048], P('dp', 'feat'), may hold values from -6 to 6
- fixed_blocks: int32 [32768, 4], P('dp', 'feat'), may hold values from 0 to 511
- fixed_coef: float32 [2048, 512], P('feat'), may hold values from -0.12 to 0.12
- member_coef: float32 [128, 256], P(('dp', 'feat')), may hold values from -0.36 to 0.36
- row_slot: int32 [32768], P(('dp', 'feat')), may hold values from 0 to 2047, as said below
- tile_source: int32 [77824], P(('dp', 'feat')), may hold values from 0 to 2048, as said below
- member_tiles: int32 [128], P(('dp', 'feat')), may hold values from 1 to 16, as said below
Outputs:
- margin: float32 [32768], P(('dp', 'feat'))
- updated_coef: float32 [128, 256], P(('dp', 'feat'))
- fixed_grad: float32 [2048, 512], P('feat')
Inputs may be any that keep to these rules, and one draw needn't show every extreme that they name: `row_slot`: each owner receives the same number of rows, 256, 128 or 64, from every device of its feat column; some owner receives 256 from every device. The rows one device sends to one owner take that owner's slots 0, 1, 2 and so on, each slot once. `tile_source`: every received row appears at exactly one position. An owner's members, in order, take consecutive runs of tiles; a member's rows fill its tiles from the first position on, and the rest of its last tile is padding, as are the tiles past all members. `member_tiles`: A member's tiles are its received rows divided by 128, rounded up; a device's members use at most 19 tiles in all, exactly 19 on the owners that receive 256 rows from every device.
All inputs are finite; a program needn't handle non-finite values. No bound on the sum of `labels` on one device may be relied on, other than what follows from the above.
Results may differ from a plain program's by a relative error of at most 0.0013.
Values may be sent and summed in bfloat16 or wider, within the bound.
No kernel may reach another device: no remote copies, remote signals or barrier semaphores. Data moves between devices by JAX's collectives and lax.ppermute only.
A program may use at most 64 MiB of HBM per device.

v0:
```python
import jax
import jax.numpy as jnp
from jax import lax
from jax.sharding import PartitionSpec as P

CG_ITERS = 2
TILE = 128
ridge_member = 1.0
ridge_fixed = 1.0
highest = lax.Precision.HIGHEST


def member_frame(tile_counts, tile_total, member_count):
    tile_ends = jnp.cumsum(tile_counts)
    positions = jnp.arange(tile_total, dtype=jnp.int32)
    member_index = jnp.sum((positions[:, None] >= tile_ends[None, :]).astype(jnp.int32), axis=1)
    return (member_index[:, None] == jnp.arange(member_count, dtype=jnp.int32)[None, :]).astype(
        jnp.float32
    )


def per_tile(tile_member, values):
    return jnp.dot(tile_member, values, precision=highest, preferred_element_type=jnp.float32)


def per_member(tile_member, values):
    return jnp.dot(tile_member.T, values, precision=highest, preferred_element_type=jnp.float32)


def row_dots(feats_wide, tile_vectors):
    return jnp.einsum("tri,ti->tr", feats_wide, tile_vectors, precision=highest)


def row_sums(row_weights, feats_wide):
    return jnp.einsum("tr,tri->ti", row_weights, feats_wide, precision=highest)


def body(
    member_feats,
    labels,
    fixed_values,
    fixed_blocks,
    fixed_coef,
    member_coef,
    row_slot,
    tile_source,
    member_tiles,
):
    dp_count = lax.axis_size("dp")
    rows_here = member_feats.shape[0]
    width = member_feats.shape[1]
    member_count = member_coef.shape[0]
    block_count = fixed_coef.shape[0]
    capacity = 2 * rows_here // dp_count
    slot_total = dp_count * capacity
    tile_total = tile_source.shape[0] // TILE
    block_index = fixed_blocks[:, 0]
    one_hot = (block_index[:, None] == jnp.arange(block_count, dtype=jnp.int32)[None, :]).astype(
        jnp.float32
    )
    looked_up = jnp.dot(one_hot, fixed_coef, precision=highest, preferred_element_type=jnp.float32)
    partial_value = jnp.sum(fixed_values.astype(jnp.float32) * looked_up, axis=1)
    fixed_score = lax.psum_scatter(partial_value, "feat", scatter_dimension=0, tiled=True)
    send_feats = jnp.zeros((slot_total, width), jnp.bfloat16).at[row_slot].set(member_feats)
    send_score = (
        jnp.zeros((slot_total,), jnp.bfloat16).at[row_slot].set(fixed_score.astype(jnp.bfloat16))
    )
    send_label = (
        jnp.zeros((slot_total,), jnp.bfloat16).at[row_slot].set(labels.astype(jnp.bfloat16))
    )
    got_feats, got_score, got_label = (
        lax.all_to_all(
            send_feats.reshape(dp_count, capacity, width),
            "dp",
            split_axis=0,
            concat_axis=0,
            tiled=True,
        ),
        lax.all_to_all(
            send_score.reshape(dp_count, capacity), "dp", split_axis=0, concat_axis=0, tiled=True
        ),
        lax.all_to_all(
            send_label.reshape(dp_count, capacity), "dp", split_axis=0, concat_axis=0, tiled=True
        ),
    )
    padded_feats = jnp.concatenate(
        [got_feats.reshape(slot_total, width), jnp.zeros((1, width), jnp.bfloat16)], axis=0
    )
    padded_score = jnp.concatenate(
        [got_score.reshape(slot_total), jnp.zeros((1,), jnp.bfloat16)], axis=0
    )
    padded_label = jnp.concatenate(
        [got_label.reshape(slot_total), jnp.zeros((1,), jnp.bfloat16)], axis=0
    )
    feats_wide = padded_feats[tile_source].astype(jnp.float32).reshape(tile_total, TILE, width)
    tile_fixed = padded_score[tile_source].astype(jnp.float32).reshape(tile_total, TILE)
    tile_label = padded_label[tile_source].astype(jnp.float32).reshape(tile_total, TILE)
    tile_member = member_frame(member_tiles, tile_total, member_count)
    logits = tile_fixed + row_dots(feats_wide, per_tile(tile_member, member_coef))
    probability = jax.nn.sigmoid(logits)
    weight = probability * (1.0 - probability)
    gradient = (
        per_member(tile_member, row_sums(tile_label - probability, feats_wide))
        - ridge_member * member_coef
    )
    diagonal = per_member(tile_member, row_sums(weight, feats_wide * feats_wide)) + ridge_member
    step_sum = jnp.zeros_like(member_coef)
    remain = gradient
    scaled = remain / diagonal
    search = scaled
    inner_product = jnp.sum(remain * scaled, axis=1)
    for iteration in range(CG_ITERS):
        projected = row_dots(feats_wide, per_tile(tile_member, search))
        image = (
            per_member(tile_member, row_sums(weight * projected, feats_wide))
            + ridge_member * search
        )
        alpha_step = inner_product / jnp.sum(search * image, axis=1)
        step_sum = step_sum + alpha_step[:, None] * search
        if iteration + 1 < CG_ITERS:
            remain = remain - alpha_step[:, None] * image
            scaled = remain / diagonal
            inner_next = jnp.sum(remain * scaled, axis=1)
            search = scaled + (inner_next / inner_product)[:, None] * search
            inner_product = inner_next
    updated_coef = member_coef + step_sum
    new_scores = row_dots(feats_wide, per_tile(tile_member, updated_coef)).reshape(-1)
    back_scores = (
        jnp.zeros((slot_total + 1,), jnp.float32).at[tile_source].set(new_scores)[:slot_total]
    )
    returned = lax.all_to_all(
        back_scores.reshape(dp_count, capacity), "dp", split_axis=0, concat_axis=0, tiled=True
    )
    member_score = returned.reshape(slot_total)[row_slot]
    margin = fixed_score + member_score
    residual = labels.astype(jnp.float32) - jax.nn.sigmoid(margin)
    group_residual = lax.all_gather(residual, "feat", axis=0, tiled=True)
    weighted_hot = one_hot * group_residual[:, None]
    contribution = jnp.dot(
        weighted_hot.T,
        fixed_values.astype(jnp.float32),
        precision=highest,
        preferred_element_type=jnp.float32,
    )
    summed = lax.psum(contribution, "dp")
    fixed_grad = ridge_fixed * fixed_coef - summed / dp_count
    return (margin, updated_coef, fixed_grad)


def solution(mesh):
    placed = (
        P(("dp", "feat"), None),
        P(("dp", "feat")),
        P("dp", "feat"),
        P("dp", "feat"),
        P("feat", None),
        P(("dp", "feat"), None),
        P(("dp", "feat")),
        P(("dp", "feat")),
        P(("dp", "feat")),
    )
    return jax.shard_map(
        body,
        mesh=mesh,
        in_specs=placed,
        out_specs=(P(("dp", "feat")), P(("dp", "feat"), None), P("feat", None)),
        check_vma=False,
    )
```

profile of v0, /device:TPU:0, one launch (start us, length us, event | category | flops | bytes accessed | tf_op | source)
XLA Modules:
  0.0 260.8 jit_solution(10872461917790779837)
XLA Ops:
  7.2 0.7 broadcast_clamp_fusion
  7.9 6.5 %copy.17 = bf16[4096,512]{0,1:T(8,128)(2,1)} copy(bf16[4096,512]{1,0:T(8,128)(2,1)} %param.11) | data formatting | bytes 8388608 | tf_op args[2]
  14.4 10.0 %multiply_reduce_fusion = f32[4096]{0:T(1024)S(1)} fusion(bf16[4096,512]{0,1:T(8,128)(2,1)} %copy.17, f32[512,512]{1,0:T(8,128)S(1)} %copy-done, s32[4096]{0:T(1024)S(1)} %bitcast.111), kind=kOutput, calls=%fused_computation.10 | convolution fusion | flops 12893286400 | bytes 5275648 | tf_op jit(solution)/shard_map/dot_general | solution.py:61
  24.4 12.7 %all-reduce.1 = f32[4096]{0:T(1024)S(1)} all-reduce(f32[4096]{0:T(1024)S(1)} %multiply_reduce_fusion), channel_id=2, replica_groups=mesh['dp'=8,'feat'=4] {'feat'}, use_global_device_ids=true, to_apply=%region_1.0.clone | all-reduce | flops 4096 | bytes 32768
  38.4 7.6 %scatter_custom_fusion.2 = bf16[2048]{0:T(1024)(128)(2,1)S(1)} fusion(s32[1024]{0:T(1024)S(1)} %get-tuple-element.10, bf16[1024]{0:T(1024)(128)(2,1)S(1)} %dynamic-slice.4, bf16[]{:T(256)} %constant.11.clone.1), kind=kCustom, calls=%fused_computation.96 | custom fusion | bytes 4098 | tf_op jit(solution)/shard_map/scatter | solution.py:66
  46.5 0.7 reduce.2
  47.2 0.6 reshape.204
  47.8 5.8 %all-to-all-start.2 = ((bf16[8,2,128]{2,1,0:T(2,128)(2,1)}), bf16[8,2,128]{2,1,0:T(2,128)(2,1)S(1)}, u32[]{:S(2)}, u32[]{:S(2)}) async-start(bf16[8,2,128]{2,1,0:T(2,128)(2,1)} %reshape.204), calls=%async_computation.2 | async-start | bytes 8192 | tf_op jit(solution)/shard_map/all_to_all | solution.py:79
  53.6 7.6 %scatter_custom_fusion.1 = bf16[2048]{0:T(1024)(128)(2,1)S(1)} fusion(s32[1024]{0:T(1024)S(1)} %get-tuple-element.10, bf16[1024]{0:T(1024)(128)(2,1)S(1)} %convert_element_type.38, bf16[]{:T(256)} %constant.11.clone.1), kind=kCustom, calls=%fused_computation.98 | custom fusion | bytes 4098 | tf_op jit(solution)/shard_map/scatter | solution.py:69
  61.2 0.7 reduce.3
  61.9 0.6 reshape.202
  62.5 6.0 %all-to-all-start.1 = ((bf16[8,2,128]{2,1,0:T(2,128)(2,1)}), bf16[8,2,128]{2,1,0:T(2,128)(2,1)S(1)}, u32[]{:S(2)}, u32[]{:S(2)}) async-start(bf16[8,2,128]{2,1,0:T(2,128)(2,1)} %reshape.202), calls=%async_computation.1 | async-start | bytes 8192 | tf_op jit(solution)/shard_map/all_to_all | solution.py:82
  68.5 6.4 %scatter_custom_fusion = bf16[2048,256]{1,0:T(8,128)(2,1)} fusion(s32[1024]{0:T(1024)S(1)} %get-tuple-element.10, bf16[1024,256]{1,0:T(8,128)(2,1)} %param.9, bf16[]{:T(256)} %constant.11.clone.1), kind=kCustom, calls=%fused_computation.31 | custom fusion | bytes 1049088 | tf_op jit(solution)/shard_map/scatter | solution.py:64
  74.9 6.1 %all-to-all-start = ((bf16[8,256,256]{2,1,0:T(8,128)(2,1)}), bf16[8,256,256]{2,1,0:T(8,128)(2,1)S(1)}, u32[]{:S(2)}, u32[]{:S(2)}) async-start(bf16[8,256,256]{2,1,0:T(8,128)(2,1)} %bitcast.1), calls=%async_computation | async-start | bytes 2097152 | tf_op jit(solution)/shard_map/all_to_all | solution.py:72
  81.9 14.7 %gather_fusion.2 = bf16[2432]{0:T(1024)(128)(2,1)S(1)} fusion(bf16[2049]{0:T(1024)(128)(2,1)S(1)} %get-tuple-element.14, s32[3072]{0:T(1024)S(1)} %pad_clamp_fusion), kind=kCustom, calls=%fused_computation.2 | custom fusion | bytes 19456 | tf_op jit(solution)/shard_map/gather | solution.py:96
  96.6 14.7 %gather_fusion.1 = bf16[2432]{0:T(1024)(128)(2,1)S(1)} fusion(bf16[2049]{0:T(1024)(128)(2,1)S(1)} %get-tuple-element.15, s32[3072]{0:T(1024)S(1)} %pad_clamp_fusion), kind=kCustom, calls=%fused_computation.1 | custom fusion | bytes 19456 | tf_op jit(solution)/shard_map/gather | solution.py:97
  111.4 7.8 %gather_fusion = bf16[2432,256]{1,0:T(8,128)(2,1)S(1)} fusion(bf16[2049,256]{1,0:T(8,128)(2,1)S(1)} %concatenate.9, s32[3072]{0:T(1024)S(1)} %pad_clamp_fusion), kind=kCustom, calls=%fused_computation | custom fusion | bytes 2500096 | tf_op jit(solution)/shard_map/gather | solution.py:95
  119.2 1.1 fusion.28
  120.3 1.4 fusion.7
  122.0 0.6 fusion.42
  123.1 1.1 fusion.26
  124.2 0.6 fusion.39
  125.7 1.1 fusion.24
  128.1 1.1 fusion.22
  129.2 12.4 %scatter_custom_fusion.3 = f32[2049]{0:T(1024)S(1)} fusion(s32[2432]{0:T(1024)S(1)} %compare_select_fusion, f32[2432]{0:T(1024)S(1)} %bitcast.110, f32[]{:T(128)} %constant.8.clone.1), kind=kCustom, calls=%fused_computation.84 | custom fusion | bytes 8200 | tf_op jit(solution)/shard_map/scatter | solution.py:129
  141.6 12.0 %all_to_all.34 = f32[8,1,256]{2,1,0:T(1,128)S(1)} all-to-all(f32[8,1,256]{2,1,0:T(1,128)S(1)} %bitcast.105), channel_id=1, replica_groups=mesh['dp'=8,'feat'=4] {'dp'}, dimensions={0} | all-to-all | bytes 16384 | tf_op jit(solution)/shard_map/all_to_all | solution.py:131
  153.6 6.1 %gather_fusion.3 = f32[1024]{0:T(1024)S(1)} fusion(f32[2048]{0:T(1024)S(1)} %bitcast.95, s32[1024]{0:T(1024)S(1)} %get-tuple-element.9), kind=kCustom, calls=%fused_computation.3 | custom fusion | bytes 12288 | tf_op jit(solution)/shard_map/gather | solution.py:134
  159.8 0.6 divide_subtract_fusion
  160.4 5.5 %all_gather.3 = f32[4096]{0:T(1024)S(1)} all-gather(f32[1024]{0:T(1024)S(1)} %get-tuple-element.5), channel_id=1, replica_groups=mesh['dp'=8,'feat'=4] {'feat'}, dimensions={0}, use_global_device_ids=true | all-gather | bytes 20480 | tf_op jit(solution)/shard_map/all_gather | solution.py:137
  165.8 11.0 %fusion = f32[512,512]{1,0:T(8,128)} fusion(bf16[4096,512]{1,0:T(8,128)(2,1)} %param.11, f32[4096]{0:T(1024)S(1)} %all_gather.3, s32[4096]{0:T(1024)S(1)} %bitcast.112), kind=kOutput, calls=%fused_computation.8 | convolution fusion | flops 12889096192 | bytes 5275648 | tf_op jit(solution)/shard_map/dot_general | solution.py:139
  176.9 74.7 %all-reduce.4.cloned.1.call-done = f32[512,512]{1,0:T(8,128)} async-done(((f32[512,512]{1,0:T(8,128)}), f32[512,512]{1,0:T(8,128)}) %all-reduce.4.cloned.1.call-update) | async-done | bytes 1048592 | tf_op jit(solution)/shard_map/psum | solution.py:145
  251.6 2.4 multiply_subtract_fusion
  (59 shorter events, 5.1 us)
Async XLA Ops:
  7.9 6.5 %copy-start = (f32[512,512]{1,0:T(8,128)S(1)}, f32[512,512]{1,0:T(8,128)}, u32[]{:S(2)}) copy-start(f32[512,512]{1,0:T(8,128)} %param.13) | copy-start | bytes 3145732
  7.9 6.5 %copy-start.5 = (s32[4096,1]{0,1:T(1,128)S(1)}, s32[4096,1]{0,1:T(1,128)}, u32[]{:S(2)}) copy-start(s32[4096,1]{0,1:T(1,128)} %param.12) | copy-start | bytes 49156
  14.4 22.7 %copy-start.7 = (u32[32]{0:T(128)S(1)}, u32[32]{0:T(128)}, u32[]{:S(2)}) copy-start(u32[32]{0:T(128)} %constant.35) | copy-start | bytes 388
  14.4 39.2 %copy-start.1 = (s32[1024]{0:T(1024)S(1)}, s32[1024]{0:T(1024)}, u32[]{:S(2)}) copy-start(s32[1024]{0:T(1024)} %param.10) | copy-start | bytes 12292
  47.8 14.7 %all-to-all-start.2 = ((bf16[8,2,128]{2,1,0:T(2,128)(2,1)}), bf16[8,2,128]{2,1,0:T(2,128)(2,1)S(1)}, u32[]{:S(2)}, u32[]{:S(2)}) async-start(bf16[8,2,128]{2,1,0:T(2,128)(2,1)} %reshape.204), calls=%async_computation.2 | async-start | bytes 8192 | tf_op jit(solution)/shard_map/all_to_all | solution.py:79
  62.5 12.4 %all-to-all-start.1 = ((bf16[8,2,128]{2,1,0:T(2,128)(2,1)}), bf16[8,2,128]{2,1,0:T(2,128)(2,1)S(1)}, u32[]{:S(2)}, u32[]{:S(2)}) async-start(bf16[8,2,128]{2,1,0:T(2,128)(2,1)} %reshape.202), calls=%async_computation.1 | async-start | bytes 8192 | tf_op jit(solution)/shard_map/all_to_all | solution.py:82
  74.9 6.4 %copy-start.6 = (s32[4]{0:T(128)S(1)}, s32[4]{0:T(128)}, u32[]{:S(2)}) copy-start(s32[4]{0:T(128)} %param.17) | copy-start | bytes 52
  74.9 6.6 %copy-start.2 = (s32[2432]{0:T(1024)S(1)}, s32[2432]{0:T(1024)}, u32[]{:S(2)}) copy-start(s32[2432]{0:T(1024)} %param.16) | copy-start | bytes 29188
  74.9 6.7 %copy-start.3 = (f32[4,256]{1,0:T(4,128)S(1)}, f32[4,256]{1,0:T(4,128)}, u32[]{:S(2)}) copy-start(f32[4,256]{1,0:T(4,128)} %param.14) | copy-start | bytes 12292
  74.9 36.5 %all-to-all-start = ((bf16[8,256,256]{2,1,0:T(8,128)(2,1)}), bf16[8,256,256]{2,1,0:T(8,128)(2,1)S(1)}, u32[]{:S(2)}, u32[]{:S(2)}) async-start(bf16[8,256,256]{2,1,0:T(8,128)(2,1)} %bitcast.1), calls=%async_computation | async-start | bytes 2097152 | tf_op jit(solution)/shard_map/all_to_all | solution.py:72
  81.0 170.6 %all-reduce.4.cloned.1.call-start = ((), (), s32[]{:S(2)}) async-start(), calls=%async_computation.4 | async-start | bytes 2097152 | tf_op jit(solution)/shard_map/psum | solution.py:145
  127.9 31.9 %copy-start.4 = (f32[4,256]{1,0:T(4,128)}, f32[4,256]{1,0:T(4,128)S(1)}, u32[]{:S(2)}) copy-start(f32[4,256]{1,0:T(4,128)S(1)} %add_add_fusion) | copy-start | bytes 12292
Sparse Core Ops, SparseCore 0:
  177.0 74.5 all-reduce.3
where the time goes:
time: 261 us
  local copies, waits for them, and re-layouts  86.3 us (33%)
  waiting for transfers between devices  74.7 us (29%)
  matrix products  30.6 us (12%)
  blocking collectives  30.2 us (12%)
  starting transfers between devices  18.2 us (7%)
  between operations  15 us (6%)
  other arithmetic  5.88 us (2%)
    psum x1, waiting for transfers between devices, body(): summed = lax.psum(contribution, 'dp')  74.7 us
    scatter x2, local copies, waits for them, and re-layouts, body(): jnp.zeros((slot_total,), jnp.bfloat16).at[row_slot]  15.2 us
    gather x1, local copies, waits for them, and re-layouts, body(): padded_score[tile_source].astype(jnp.float32).reshape(tile_total, TILE)  14.7 us
    gather x1, local copies, waits for them, and re-layouts, body(): padded_label[tile_source].astype(jnp.float32).reshape(tile_total, TILE)  14.7 us
    unnamed x1, blocking collectives  12.7 us
    scatter x1, local copies, waits for them, and re-layouts, body(): jnp.zeros((slot_total + 1,), jnp.float32).at[tile_source].set(new_scores)  12.4 us
    all_to_all x1, blocking collectives, body(): lax.all_to_all(back_scores.reshape(dp_count, capacity), 'dp', split_axis=...  12 us
    dot_general x1, matrix products, body(): jnp.dot(weighted_hot.T, fixed_values.astype(jnp.float32), precision=highe...  11 us
  transfers between devices with their start and end apart: 4, of which 1 were waited for; matrix products, arithmetic and copies ran while one was open for 17% of the time, Pallas kernels for 0%

commit v1 on v0

--- a/solution.py
+++ b/solution.py
@@ -142,7 +142,8 @@
         precision=highest,
         preferred_element_type=jnp.float32,
     )
-    summed = lax.psum(contribution, "dp")
+    shards = lax.all_gather(contribution, "dp")
+    summed = jnp.sum(shards, axis=0)
     fixed_grad = ridge_fixed * fixed_coef - summed / dp_count
     return (margin, updated_coef, fixed_grad)
 

time: 261 us -> 312 us (1.20)
  waiting for transfers between devices: 74.7 us -> 122 us
  other arithmetic: 5.88 us -> 9.85 us
    all_gather x0 -> x1, waiting for transfers between devices: none -> 122 us  [body(): shards = lax.all_gather(contribution, 'dp')]
    psum x1 -> x0, waiting for transfers between devices: 74.7 us -> none  [body(): summed = lax.psum(contribution, 'dp')]
    reduce_sum x0 -> x1, other arithmetic: none -> 4.49 us  [body(): summed = jnp.sum(shards, axis=0)]
  transfers between devices with their start and end apart: 4 -> 4, of which waited for: 1 -> 1; matrix products, arithmetic and copies ran while one was open for 17% -> 20% of each run, Pallas kernels for 0% -> 0%
where the time goes in v1:
time: 312 us; the launch traced here: 311 us
  waiting for transfers between devices  122 us (39%)
  local copies, waits for them, and re-layouts  86.2 us (28%)
  matrix products  30.7 us (10%)
  blocking collectives  28.2 us (9%)
  starting transfers between devices  19.4 us (6%)
  between operations  15 us (5%)
  other arithmetic  9.85 us (3%)
    all_gather x1, waiting for transfers between devices, body(): shards = lax.all_gather(contribution, 'dp')  122 us
    scatter x2, local copies, waits for them, and re-layouts, body(): jnp.zeros((slot_total,), jnp.bfloat16).at[row_slot]  15.2 us
    gather x1, local copies, waits for them, and re-layouts, body(): padded_label[tile_source].astype(jnp.float32).reshape(tile_total, TILE)  14.7 us
    gather x1, local copies, waits for them, and re-layouts, body(): padded_score[tile_source].astype(jnp.float32).reshape(tile_total, TILE)  14.7 us
    scatter x1, local copies, waits for them, and re-layouts, body(): jnp.zeros((slot_total + 1,), jnp.float32).at[tile_source].set(new_scores)  12.4 us
    all_to_all x1, blocking collectives, body(): lax.all_to_all(back_scores.reshape(dp_count, capacity), 'dp', split_axis=...  12 us
    dot_general x1, matrix products, body(): jnp.dot(weighted_hot.T, fixed_values.astype(jnp.float32), precision=highe...  11 us
    unnamed x1, blocking collectives  10.7 us
  transfers between devices with their start and end apart: 4, of which 1 were waited for; matrix products, arithmetic and copies ran while one was open for 20% of the time, Pallas kernels for 0%

profile of v1, /device:TPU:0, one launch (start us, length us, event | category | flops | bytes accessed | tf_op | source)
XLA Modules:
  0.0 311.2 jit_solution(16000938620939031829)
XLA Ops:
  7.2 0.7 convert_element_type.38
  7.9 0.7 broadcast_clamp_fusion
  8.5 7.6 %scatter_custom_fusion.1 = bf16[2048]{0:T(1024)(128)(2,1)S(1)} fusion(s32[1024]{0:T(1024)S(1)} %get-tuple-element.10, bf16[1024]{0:T(1024)(128)(2,1)S(1)} %convert_element_type.38, bf16[]{:T(256)} %constant.11.clone.1), kind=kCustom, calls=%fused_computation.98 | custom fusion | bytes 4098 | tf_op jit(solution)/shard_map/scatter | solution.py:69
  16.7 0.7 reduce.3
  17.3 0.6 reshape.203
  17.9 7.3 %all-to-all-start.1 = ((bf16[8,2,128]{2,1,0:T(2,128)(2,1)}), bf16[8,2,128]{2,1,0:T(2,128)(2,1)S(1)}, u32[]{:S(2)}, u32[]{:S(2)}) async-start(bf16[8,2,128]{2,1,0:T(2,128)(2,1)} %reshape.203), calls=%async_computation.1 | async-start | bytes 8192 | tf_op jit(solution)/shard_map/all_to_all | solution.py:82
  25.2 6.5 %copy.17 = bf16[4096,512]{0,1:T(8,128)(2,1)} copy(bf16[4096,512]{1,0:T(8,128)(2,1)} %param.11) | data formatting | bytes 8388608 | tf_op args[2]
  31.8 10.1 %multiply_reduce_fusion = f32[4096]{0:T(1024)S(1)} fusion(bf16[4096,512]{0,1:T(8,128)(2,1)} %copy.17, f32[512,512]{1,0:T(8,128)S(1)} %copy-done, s32[4096]{0:T(1024)S(1)} %bitcast.117), kind=kOutput, calls=%fused_computation.10 | convolution fusion | flops 12893286400 | bytes 5275648 | tf_op jit(solution)/shard_map/dot_general | solution.py:61
  41.9 10.7 %all-reduce.1 = f32[4096]{0:T(1024)S(1)} all-reduce(f32[4096]{0:T(1024)S(1)} %multiply_reduce_fusion), channel_id=3, replica_groups=mesh['dp'=8,'feat'=4] {'feat'}, use_global_device_ids=true, to_apply=%region_1.0.clone | all-reduce | flops 4096 | bytes 32768
  53.8 7.6 %scatter_custom_fusion.2 = bf16[2048]{0:T(1024)(128)(2,1)S(1)} fusion(s32[1024]{0:T(1024)S(1)} %get-tuple-element.10, bf16[1024]{0:T(1024)(128)(2,1)S(1)} %dynamic-slice.4, bf16[]{:T(256)} %constant.11.clone.1), kind=kCustom, calls=%fused_computation.96 | custom fusion | bytes 4098 | tf_op jit(solution)/shard_map/scatter | solution.py:66
  61.4 0.7 reduce.2
  62.1 0.6 reshape.205
  62.7 5.7 %all-to-all-start.2 = ((bf16[8,2,128]{2,1,0:T(2,128)(2,1)}), bf16[8,2,128]{2,1,0:T(2,128)(2,1)S(1)}, u32[]{:S(2)}, u32[]{:S(2)}) async-start(bf16[8,2,128]{2,1,0:T(2,128)(2,1)} %reshape.205), calls=%async_computation.2 | async-start | bytes 8192 | tf_op jit(solution)/shard_map/all_to_all | solution.py:79
  68.4 6.4 %scatter_custom_fusion = bf16[2048,256]{1,0:T(8,128)(2,1)} fusion(s32[1024]{0:T(1024)S(1)} %get-tuple-element.10, bf16[1024,256]{1,0:T(8,128)(2,1)} %param.9, bf16[]{:T(256)} %constant.11.clone.1), kind=kCustom, calls=%fused_computation.31 | custom fusion | bytes 1049088 | tf_op jit(solution)/shard_map/scatter | solution.py:64
  74.8 6.1 %all-to-all-start = ((bf16[8,256,256]{2,1,0:T(8,128)(2,1)}), bf16[8,256,256]{2,1,0:T(8,128)(2,1)S(1)}, u32[]{:S(2)}, u32[]{:S(2)}) async-start(bf16[8,256,256]{2,1,0:T(8,128)(2,1)} %bitcast.1), calls=%async_computation | async-start | bytes 2097152 | tf_op jit(solution)/shard_map/all_to_all | solution.py:72
  81.8 14.7 %gather_fusion.2 = bf16[2432]{0:T(1024)(128)(2,1)S(1)} fusion(bf16[2049]{0:T(1024)(128)(2,1)S(1)} %get-tuple-element.14, s32[3072]{0:T(1024)S(1)} %pad_clamp_fusion), kind=kCustom, calls=%fused_computation.2 | custom fusion | bytes 19456 | tf_op jit(solution)/shard_map/gather | solution.py:96
  96.5 14.7 %gather_fusion.1 = bf16[2432]{0:T(1024)(128)(2,1)S(1)} fusion(bf16[2049]{0:T(1024)(128)(2,1)S(1)} %get-tuple-element.15, s32[3072]{0:T(1024)S(1)} %pad_clamp_fusion), kind=kCustom, calls=%fused_computation.1 | custom fusion | bytes 19456 | tf_op jit(solution)/shard_map/gather | solution.py:97
  111.3 7.8 %gather_fusion = bf16[2432,256]{1,0:T(8,128)(2,1)S(1)} fusion(bf16[2049,256]{1,0:T(8,128)(2,1)S(1)} %concatenate.9, s32[3072]{0:T(1024)S(1)} %pad_clamp_fusion), kind=kCustom, calls=%fused_computation | custom fusion | bytes 2500096 | tf_op jit(solution)/shard_map/gather | solution.py:95
  119.1 1.1 fusion.28
  120.2 1.4 fusion.7
  121.9 0.6 fusion.42
  123.0 1.1 fusion.26
  125.6 1.1 fusion.24
  128.0 1.1 fusion.22
  129.1 12.4 %scatter_custom_fusion.3 = f32[2049]{0:T(1024)S(1)} fusion(s32[2432]{0:T(1024)S(1)} %compare_select_fusion, f32[2432]{0:T(1024)S(1)} %bitcast.116, f32[]{:T(128)} %constant.8.clone.1), kind=kCustom, calls=%fused_computation.84 | custom fusion | bytes 8200 | tf_op jit(solution)/shard_map/scatter | solution.py:129
  141.5 12.0 %all_to_all.34 = f32[8,1,256]{2,1,0:T(1,128)S(1)} all-to-all(f32[8,1,256]{2,1,0:T(1,128)S(1)} %bitcast.111), channel_id=1, replica_groups=mesh['dp'=8,'feat'=4] {'dp'}, dimensions={0} | all-to-all | bytes 16384 | tf_op jit(solution)/shard_map/all_to_all | solution.py:131
  153.5 6.1 %gather_fusion.3 = f32[1024]{0:T(1024)S(1)} fusion(f32[2048]{0:T(1024)S(1)} %bitcast.100, s32[1024]{0:T(1024)S(1)} %get-tuple-element.9), kind=kCustom, calls=%fused_computation.3 | custom fusion | bytes 12288 | tf_op jit(solution)/shard_map/gather | solution.py:134
  160.3 5.5 %all_gather.9 = f32[4096]{0:T(1024)S(1)} all-gather(f32[1024]{0:T(1024)S(1)} %get-tuple-element.5), channel_id=1, replica_groups=mesh['dp'=8,'feat'=4] {'feat'}, dimensions={0}, use_global_device_ids=true | all-gather | bytes 20480 | tf_op jit(solution)/shard_map/all_gather | solution.py:137
  165.8 11.0 %fusion = f32[512,512]{1,0:T(8,128)} fusion(bf16[4096,512]{1,0:T(8,128)(2,1)} %param.11, f32[4096]{0:T(1024)S(1)} %all_gather.9, s32[4096]{0:T(1024)S(1)} %bitcast.118), kind=kOutput, calls=%fused_computation.8 | convolution fusion | flops 12889096192 | bytes 5275648 | tf_op jit(solution)/shard_map/dot_general | solution.py:139
  176.8 121.8 %all-gather.3.cloned.1.call-done = f32[4096,512]{1,0:T(8,128)} async-done(((f32[512,512]{1,0:T(8,128)}), f32[4096,512]{1,0:T(8,128)}) %all-gather.3.cloned.1.call-update) | async-done | bytes 8388624 | tf_op jit(solution)/shard_map/all_gather | solution.py:145
  298.6 4.5 %reduce_sum.69 = f32[512,512]{1,0:T(8,128)S(1)} reduce(f32[8,512,512]{2,1,0:T(8,128)} %bitcast.109, f32[]{:T(128)} %constant.8.clone.1), dimensions={0}, to_apply=%region_12.13 | reduce | flops 1835008 | bytes 9437188 | tf_op jit(solution)/shard_map/reduce_sum | solution.py:146
  303.1 1.2 multiply_subtract_fusion
  (60 shorter events, 6.3 us)
Async XLA Ops:
  17.9 44.7 %all-to-all-start.1 = ((bf16[8,2,128]{2,1,0:T(2,128)(2,1)}), bf16[8,2,128]{2,1,0:T(2,128)(2,1)S(1)}, u32[]{:S(2)}, u32[]{:S(2)}) async-start(bf16[8,2,128]{2,1,0:T(2,128)(2,1)} %reshape.203), calls=%async_computation.1 | async-start | bytes 8192 | tf_op jit(solution)/shard_map/all_to_all | solution.py:82
  25.2 6.5 %copy-start = (f32[512,512]{1,0:T(8,128)S(1)}, f32[512,512]{1,0:T(8,128)}, u32[]{:S(2)}) copy-start(f32[512,512]{1,0:T(8,128)} %param.13) | copy-start | bytes 3145732
  25.2 6.5 %copy-start.5 = (s32[4096,1]{0,1:T(1,128)S(1)}, s32[4096,1]{0,1:T(1,128)}, u32[]{:S(2)}) copy-start(s32[4096,1]{0,1:T(1,128)} %param.12) | copy-start | bytes 49156
  31.8 20.8 %copy-start.7 = (u32[32]{0:T(128)S(1)}, u32[32]{0:T(128)}, u32[]{:S(2)}) copy-start(u32[32]{0:T(128)} %constant.35) | copy-start | bytes 388
  62.7 12.1 %all-to-all-start.2 = ((bf16[8,2,128]{2,1,0:T(2,128)(2,1)}), bf16[8,2,128]{2,1,0:T(2,128)(2,1)S(1)}, u32[]{:S(2)}, u32[]{:S(2)}) async-start(bf16[8,2,128]{2,1,0:T(2,128)(2,1)} %reshape.205), calls=%async_computation.2 | async-start | bytes 8192 | tf_op jit(solution)/shard_map/all_to_all | solution.py:79
  74.8 6.4 %copy-start.6 = (s32[4]{0:T(128)S(1)}, s32[4]{0:T(128)}, u32[]{:S(2)}) copy-start(s32[4]{0:T(128)} %param.17) | copy-start | bytes 52
  74.8 6.6 %copy-start.2 = (s32[2432]{0:T(1024)S(1)}, s32[2432]{0:T(1024)}, u32[]{:S(2)}) copy-start(s32[2432]{0:T(1024)} %param.16) | copy-start | bytes 29188
  74.8 6.7 %copy-start.3 = (f32[4,256]{1,0:T(4,128)S(1)}, f32[4,256]{1,0:T(4,128)}, u32[]{:S(2)}) copy-start(f32[4,256]{1,0:T(4,128)} %param.14) | copy-start | bytes 12292
  74.8 36.5 %all-to-all-start = ((bf16[8,256,256]{2,1,0:T(8,128)(2,1)}), bf16[8,256,256]{2,1,0:T(8,128)(2,1)S(1)}, u32[]{:S(2)}, u32[]{:S(2)}) async-start(bf16[8,256,256]{2,1,0:T(8,128)(2,1)} %bitcast.1), calls=%async_computation | async-start | bytes 2097152 | tf_op jit(solution)/shard_map/all_to_all | solution.py:72
  80.9 217.7 %all-gather.3.cloned.1.call-start = ((), (), s32[]{:S(2)}) async-start(), calls=%async_computation.4 | async-start | bytes 9437184 | tf_op jit(solution)/shard_map/all_gather | solution.py:145
  127.8 31.9 %copy-start.4 = (f32[4,256]{1,0:T(4,128)}, f32[4,256]{1,0:T(4,128)S(1)}, u32[]{:S(2)}) copy-start(f32[4,256]{1,0:T(4,128)S(1)} %add_add_fusion) | copy-start | bytes 12292
  153.5 6.2 %copy-start.1 = (s32[1024]{0:T(1024)S(1)}, s32[1024]{0:T(1024)}, u32[]{:S(2)}) copy-start(s32[1024]{0:T(1024)} %param.10) | copy-start | bytes 12292
Sparse Core Ops, SparseCore 0:
  176.9 121.6 all-gather.2
